TPU v7x, 32 devices: a whole 2x2x4 slice. The times are simulated.
32 devices in a mesh: groups: 2 (over y), expert: 8 (over z, core), sub: 2 (over x).
Axes of the slice: x: 2, y: 2, z: 4, core: 2. Of those that a mesh axis runs over, the one named last changes fastest.
Arguments:
- latent: bfloat16 [4096, 1024], P(('groups', 'expert', 'sub')), parts along dimension 0, may hold values from -6 to 6
- routes: int32 [4096, 4], P(('groups', 'expert', 'sub')), parts along dimension 0, may hold values from 0 to 7, all different within a row; in each aligned block of 128 rows (0 to 127, 128 to 255, ...) at most 96 rows name the same one
- gates: float32 [4096, 4], P(('groups', 'expert', 'sub')), parts along dimension 0, may hold values from 0.1 to 1
- up_weight: bfloat16 [8, 1024, 2688], P('expert', None, 'sub'), may hold values from -0.1875 to 0.1875
- down_weight: bfloat16 [8, 1024, 2688], P('expert', None, 'sub'), may hold values from -0.125 to 0.125
Outputs:
- mixed: bfloat16 [4096, 1024], P(('groups', 'expert', 'sub')), parts along dimension 0
There are 2 independent parts, one for each index of `groups`. A program takes and returns all parts, laid end to end along the dimension named above; an argument that names none is the same for every part. Nothing has to cross between parts.
Inputs may be any that keep to these rules, and one draw needn't show every extreme that they name: `routes`: each token names 4 different experts; among the 128 tokens of one device no expert is named more than 96 times, a bound that some block reaches.
All inputs are finite; a program needn't handle non-finite values.
Results may differ from a plain program's by a relative error of at most 0.0058.
Values may be sent and summed in bfloat16 or wider, within the bound.
A program may use at most 128 MiB of HBM per device.

v0:
```python
import jax
import jax.numpy as jnp
from jax import lax
from jax.sharding import PartitionSpec as P


def expert_part(row_block, up_part, down_part):
    preact = jnp.dot(row_block, up_part, preferred_element_type=jnp.float32)
    active = jnp.square(jnp.maximum(preact, 0.0)).astype(jnp.bfloat16)
    return lax.dot_general(
        active, down_part, (((1,), (1,)), ((), ())), preferred_element_type=jnp.float32
    )


def local(latent, routes, gates, up_weight, down_weight):
    tokens_here, row_width = latent.shape
    top_count = routes.shape[1]
    experts = lax.axis_size("expert")
    slot_most = min(tokens_here, 3 * tokens_here * top_count // (2 * experts))
    pair_count = tokens_here * top_count
    route_ids = routes.reshape(-1)
    one_hot = (route_ids[:, None] == jnp.arange(experts, dtype=jnp.int32)[None, :]).astype(
        jnp.int32
    )
    before = jnp.cumsum(one_hot, axis=0) - one_hot
    slot_rank = jnp.sum(before * one_hot, axis=1)
    slot_of = route_ids * slot_most + slot_rank
    source = (
        jnp.full((experts * slot_most,), pair_count, jnp.int32)
        .at[slot_of]
        .set(jnp.arange(pair_count, dtype=jnp.int32))
    )
    padded = jnp.concatenate([latent, jnp.zeros((1, row_width), latent.dtype)], axis=0)
    send_rows = padded[source // top_count].reshape(experts, slot_most, row_width)
    arrived = lax.all_to_all(send_rows, "expert", split_axis=0, concat_axis=0, tiled=True)
    flat_rows = arrived.reshape(-1, row_width)
    summed = expert_part(
        flat_rows,
        lax.all_gather(up_weight, "sub", axis=2, tiled=True)[0],
        lax.all_gather(down_weight, "sub", axis=2, tiled=True)[0],
    )
    expert_out = lax.all_to_all(
        summed.astype(jnp.bfloat16).reshape(arrived.shape),
        "expert",
        split_axis=0,
        concat_axis=0,
        tiled=True,
    )
    values = expert_out.reshape(experts * slot_most, row_width)[slot_of].astype(jnp.float32)
    mixed_out = jnp.sum(
        values.reshape(tokens_here, top_count, row_width) * gates[:, :, None], axis=1
    )
    return mixed_out.astype(jnp.bfloat16)


def solution(mesh):
    placed = (
        P(("groups", "expert", "sub"), None),
        P(("groups", "expert", "sub"), None),
        P(("groups", "expert", "sub"), None),
        P("expert", None, "sub"),
        P("expert", None, "sub"),
    )
    return jax.shard_map(
        local,
        mesh=mesh,
        in_specs=placed,
        out_specs=P(("groups", "expert", "sub"), None),
        check_vma=False,
    )
```

profile of v0, /device:TPU:0, one launch (start us, length us, event | category | flops | bytes accessed | tf_op | source)
XLA Modules:
  0.0 220.0 jit_solution(8751266270399759051)
XLA Ops:
  6.5 0.7 all-gather.3.cloned.1.call-update
  7.3 0.0 all-gather.5.cloned.1.call-start
  7.3 0.7 all-gather.5.cloned.1.call-update
  8.0 0.1 copy.8
  8.1 0.1 eq.29
  8.2 0.1 eq.25
  8.4 1.1 reduce-window.6
  9.5 0.2 slice_reduce_fusion
  9.8 0.1 copy.7
  9.9 0.1 mul.29
  10.0 0.1 fusion.7
  10.1 2.4 %scatter_custom_fusion = s32[768]{0:T(1024)S(1)} fusion(s32[512]{0:T(512)S(1)} %bitcast.27, s32[512]{0:T(512)S(1)} %iota.11, s32[]{:T(128)} %constant.13.clone.1), kind=kCustom, calls=%fused_computation.27 | custom fusion | bytes 3076 | tf_op jit(solution)/shard_map/scatter | solution.py:31
  12.6 2.8 %gather_fusion = bf16[768,1024]{1,0:T(8,128)(2,1)S(1)} fusion(bf16[129,1024]{1,0:T(8,128)(2,1)S(1)} %concatenate.3, s32[1024]{0:T(1024)S(1)} %pad_clamp_fusion.1), kind=kCustom, calls=%fused_computation | custom fusion | bytes 3148800 | tf_op jit(solution)/shard_map/gather | solution.py:34
  15.5 43.9 %all_to_all.10 = bf16[8,96,1024]{2,1,0:T(8,128)(2,1)S(1)} all-to-all(bf16[8,96,1024]{2,1,0:T(8,128)(2,1)S(1)} %bitcast.25), channel_id=1, replica_groups=mesh['groups'=2,'expert'=8,'sub'=2] {'expert'}, dimensions={0} | all-to-all | bytes 3145728 | tf_op jit(solution)/shard_map/all_to_all | solution.py:35
  59.4 23.7 %all-gather.3.cloned.1.call-done = bf16[1,1024,2688]{1,2,0:T(8,128)(2,1)} async-done(((bf16[1,1024,1344]{1,2,0:T(8,128)(2,1)}), bf16[1,1024,2688]{1,2,0:T(8,128)(2,1)}) %all-gather.3.cloned.1.call-update) | async-done | bytes 5505040 | tf_op jit(solution)/shard_map/all_gather | solution.py:39
  83.1 8.8 %multiply_convert_fusion = bf16[768,2688]{1,0:T(8,128)(2,1)} fusion(bf16[768,1024]{1,0:T(8,128)(2,1)S(1)} %bitcast.26, bf16[1,1024,2688]{1,2,0:T(8,128)(2,1)} %all-gather.3.cloned.1.call-done), kind=kOutput, calls=%fused_computation.3 | convolution fusion | flops 4234051584 | bytes 11206656 | tf_op jit(solution)/shard_map/dot_general | solution.py:8
  91.9 64.3 %all-gather.5.cloned.1.call-done = bf16[1,1024,2688]{1,2,0:T(8,128)(2,1)} async-done(((bf16[1,1024,1344]{1,2,0:T(8,128)(2,1)}), bf16[1,1024,2688]{1,2,0:T(8,128)(2,1)}) %all-gather.5.cloned.1.call-update) | async-done | bytes 5505040 | tf_op jit(solution)/shard_map/all_gather | solution.py:40
  156.2 9.6 %fusion.3 = bf16[768,1024]{1,0:T(8,128)(2,1)} fusion(bf16[768,2688]{1,0:T(8,128)(2,1)} %multiply_convert_fusion, bf16[1,1024,2688]{1,2,0:T(8,128)(2,1)} %all-gather.5.cloned.1.call-done), kind=kOutput, calls=%fused_computation.8 | convolution fusion | flops 4228644864 | bytes 11206656 | tf_op jit(solution)/shard_map/dot_general | solution.py:10
  165.8 4.7 %all-to-all-start.1 = ((bf16[8,96,1024]{2,1,0:T(8,128)(2,1)}), bf16[8,96,1024]{2,1,0:T(8,128)(2,1)S(1)}, u32[]{:S(2)}, u32[]{:S(2)}) async-start(bf16[8,96,1024]{2,1,0:T(8,128)(2,1)} %bitcast.8), calls=%async_computation.1 | async-start | bytes 3145728 | tf_op jit(solution)/shard_map/all_to_all | solution.py:42
  170.6 0.1 copy.10
  170.7 37.7 %all-to-all-done.1 = bf16[8,96,1024]{2,1,0:T(8,128)(2,1)S(1)} async-done(((bf16[8,96,1024]{2,1,0:T(8,128)(2,1)}), bf16[8,96,1024]{2,1,0:T(8,128)(2,1)S(1)}, u32[]{:S(2)}, u32[]{:S(2)}) %all-to-all-start.1) | async-done | bytes 1572896 | tf_op jit(solution)/shard_map/all_to_all | solution.py:42
  208.4 2.0 gather_fusion.1
  210.4 0.7 reshape.68
  211.1 2.1 multiply_reduce_fusion
  (17 shorter events, 0.1 us)
Async XLA Ops:
  6.5 1.5 copy-start.1
  6.5 3.5 %copy-start = (bf16[128,1024]{1,0:T(8,128)(2,1)S(1)}, bf16[128,1024]{1,0:T(8,128)(2,1)}, u32[]{:S(2)}) copy-start(bf16[128,1024]{1,0:T(8,128)(2,1)} %param.5) | copy-start | bytes 786436
  6.5 76.6 %all-gather.3.cloned.1.call-start = ((), (), s32[]{:S(2)}) async-start(), calls=%async_computation.2 | async-start | bytes 8257536 | tf_op jit(solution)/shard_map/all_gather | solution.py:39
  7.3 149.0 %all-gather.5.cloned.1.call-start = ((), (), s32[]{:S(2)}) async-start(), calls=%async_computation.3 | async-start | bytes 8257536 | tf_op jit(solution)/shard_map/all_gather | solution.py:40
  165.8 4.7 %copy-start.2 = (f32[128,4]{0,1:T(4,128)S(1)}, f32[128,4]{0,1:T(4,128)}, u32[]{:S(2)}) copy-start(f32[128,4]{0,1:T(4,128)} %param.7) | copy-start | bytes 6148
  165.8 42.5 %all-to-all-start.1 = ((bf16[8,96,1024]{2,1,0:T(8,128)(2,1)}), bf16[8,96,1024]{2,1,0:T(8,128)(2,1)S(1)}, u32[]{:S(2)}, u32[]{:S(2)}) async-start(bf16[8,96,1024]{2,1,0:T(8,128)(2,1)} %bitcast.8), calls=%async_computation.1 | async-start | bytes 3145728 | tf_op jit(solution)/shard_map/all_to_all | solution.py:42
Sparse Core Ops, SparseCore 0:
  8.9 74.2 all-gather.2
  84.7 71.4 all-gather.4
where the time goes:
time: 220 us
  waiting for transfers between devices  127 us (58%)
  blocking collectives  43.9 us (20%)
  matrix products  18.4 us (8%)
  between operations  13.5 us (6%)
  local copies, waits for them, and re-layouts  8.93 us (4%)
  starting transfers between devices  4.78 us (2%)
  other arithmetic  3.39 us (2%)
    all_gather x1, waiting for transfers between devices, local(): lax.all_gather(down_weight, 'sub', axis=2, tiled=True)[0]  64.3 us
    all_to_all x1, blocking collectives, local(): lax.all_to_all(send_rows, 'expert', split_axis=0, concat_axis=0, tiled=True)  43.9 us
    all_to_all x1, waiting for transfers between devices, local(): lax.all_to_all(summed.astype(jnp.bfloat16).reshape(arrived.shape), 'exper...  37.7 us
    all_gather x1, waiting for transfers between devices, local(): lax.all_gather(up_weight, 'sub', axis=2, tiled=True)[0]  23.7 us
    dot_general x1, matrix products, expert_part(): lax.dot_general(active, down_part, (((1,), (1,)), ((), ())), preferred_el...  9.62 us
    dot_general x1, matrix products, expert_part(): preact = jnp.dot(row_block, up_part, preferred_element_type=jnp.float32)  8.77 us
    all_to_all x1, starting transfers between devices, local(): lax.all_to_all(summed.astype(jnp.bfloat16).reshape(arrived.shape), 'exper...  4.74 us
  transfers between devices with their start and end apart: 3, of which 3 were waited for; matrix products, arithmetic and copies ran while one was open for 7% of the time, Pallas kernels for 0%

commit v1 on v0

--- a/solution.py
+++ b/solution.py
@@ -2,6 +2,13 @@
 import jax.numpy as jnp
 from jax import lax
 from jax.sharding import PartitionSpec as P
+
+
+def gather_over(x, axis, dim):
+    size = lax.axis_size(axis)
+    blocks = jnp.stack([x for _ in range(size)])
+    blocks = lax.all_to_all(blocks, axis, split_axis=0, concat_axis=0)
+    return jnp.concatenate(blocks, axis=dim)
 
 
 def expert_part(row_block, up_part, down_part):
@@ -36,7 +43,7 @@
     flat_rows = arrived.reshape(-1, row_width)
     summed = expert_part(
         flat_rows,
-        lax.all_gather(up_weight, "sub", axis=2, tiled=True)[0],
+        gather_over(up_weight, "sub", 2)[0],
         lax.all_gather(down_weight, "sub", axis=2, tiled=True)[0],
     )
     expert_out = lax.all_to_all(

time: 220 us -> 230 us (1.045)
  waiting for transfers between devices: 127 us -> 72.6 us
  blocking collectives: 43.9 us -> 96.2 us
  starting transfers between devices: 4.78 us -> 11.3 us
  other arithmetic: 3.39 us -> 6.98 us
  local copies, waits for them, and re-layouts: 8.93 us -> 11.3 us
    all_gather x1, waiting for transfers between devices: 64.3 us -> 0.01 us  [local(): lax.all_gather(down_weight, 'sub', axis=2, tiled=True)[0]]
    all_to_all x1, blocking collectives: 43.9 us -> 96.2 us  [gather_over(): blocks = lax.all_to_all(blocks, axis, split_axis=0, concat_axis=0)]
    all_to_all x0 -> x1, waiting for transfers between devices: none -> 34.2 us  [local(): lax.all_to_all(send_rows, 'expert', split_axis=0, concat_axis=0, tiled=True)]
    all_gather x1 -> x0, waiting for transfers between devices: 23.7 us -> none  [local(): lax.all_gather(up_weight, 'sub', axis=2, tiled=True)[0]]
    all_to_all x0 -> x1, starting transfers between devices: none -> 6.62 us  [local(): lax.all_to_all(send_rows, 'expert', split_axis=0, concat_axis=0, tiled=True)]
    another operation x2 -> x3, other arithmetic: 1.18 us -> 4.09 us  [the longest x1 2.93 us: gather_over(): blocks = jnp.stack([x for _ in range(size)])]
  transfers between devices with their start and end apart: 3 -> 3, of which waited for: 3 -> 2; matrix products, arithmetic and copies ran while one was open for 7% -> 5% of each run, Pallas kernels for 0% -> 0%
where the time goes in v1:
time: 230 us; the launch traced here: 229 us
  blocking collectives  96.2 us (42%)
  waiting for transfers between devices  72.6 us (32%)
  matrix products  17.7 us (8%)
  between operations  13.5 us (6%)
  local copies, waits for them, and re-layouts  11.3 us (5%)
  starting transfers between devices  11.3 us (5%)
  other arithmetic  6.98 us (3%)
    all_to_all x1, blocking collectives, gather_over(): blocks = lax.all_to_all(blocks, axis, split_axis=0, concat_axis=0)  96.2 us
    all_to_all x1, waiting for transfers between devices, local(): lax.all_to_all(summed.astype(jnp.bfloat16).reshape(arrived.shape), 'exper...  37.7 us
    all_to_all x1, waiting for transfers between devices, local(): lax.all_to_all(send_rows, 'expert', split_axis=0, concat_axis=0, tiled=True)  34.2 us
    dot_general x1, matrix products, expert_part(): lax.dot_general(active, down_part, (((1,), (1,)), ((), ())), preferred_el...  9.6 us
    dot_general x1, matrix products, expert_part(): preact = jnp.dot(row_block, up_part, preferred_element_type=jnp.float32)  8.13 us
    all_to_all x1, starting transfers between devices, local(): lax.all_to_all(send_rows, 'expert', split_axis=0, concat_axis=0, tiled=True)  6.62 us
    all_to_all x1, starting transfers between devices, local(): lax.all_to_all(summed.astype(jnp.bfloat16).reshape(arrived.shape), 'exper...  4.6 us
  transfers between devices with their start and end apart: 3, of which 2 were waited for; matrix products, arithmetic and copies ran while one was open for 5% of the time, Pallas kernels for 0%

profile of v1, /device:TPU:0, one launch (start us, length us, event | category | flops | bytes accessed | tf_op | source)
XLA Modules:
  0.0 229.5 jit_solution(6000950186432391372)
XLA Ops:
  6.5 0.8 copy.8
  7.3 0.1 eq.29
  7.4 0.1 eq.25
  7.5 0.7 broadcast_multiply_fusion
  8.2 1.1 reduce-window.6
  9.4 0.2 slice_reduce_fusion
  9.6 0.1 copy.7
  9.7 0.1 mul.29
  10.0 2.4 %scatter_custom_fusion = s32[768]{0:T(1024)S(1)} fusion(s32[512]{0:T(512)S(1)} %bitcast.29, s32[512]{0:T(512)S(1)} %iota.11, s32[]{:T(128)} %constant.13.clone.1), kind=kCustom, calls=%fused_computation.27 | custom fusion | bytes 3076 | tf_op jit(solution)/shard_map/scatter | solution.py:38
  12.4 1.0 concatenate.3
  13.4 3.6 %gather_fusion = bf16[768,1024]{1,0:T(8,128)(2,1)} fusion(bf16[129,1024]{1,0:T(8,128)(2,1)S(1)} %concatenate.3, s32[1024]{0:T(1024)S(1)} %pad_clamp_fusion.1), kind=kCustom, calls=%fused_computation | custom fusion | bytes 3148800 | tf_op jit(solution)/shard_map/gather | solution.py:41
  17.0 6.6 %all-to-all-start = ((bf16[8,96,1024]{2,1,0:T(8,128)(2,1)}), bf16[8,96,1024]{2,1,0:T(8,128)(2,1)}, u32[]{:S(2)}, u32[]{:S(2)}) async-start(bf16[8,96,1024]{2,1,0:T(8,128)(2,1)} %bitcast.4), calls=%async_computation | async-start | bytes 3145728 | tf_op jit(solution)/shard_map/all_to_all | solution.py:42
  23.7 0.7 all-gather.2.cloned.1.call-update
  24.4 2.9 %pad_maximum_fusion = bf16[2,1,1024,1344]{2,3,1,0:T(8,128)(2,1)} fusion(bf16[1,1,1024,1344]{2,3,1,0:T(8,128)(2,1)S(1)} %bitcast.28), kind=kLoop, calls=%fused_computation.4 | loop fusion | flops 2752512 | bytes 8257536 | tf_op jit(solution)/shard_map/stack | solution.py:9
  27.3 34.2 %all-to-all-done = bf16[8,96,1024]{2,1,0:T(8,128)(2,1)} async-done(((bf16[8,96,1024]{2,1,0:T(8,128)(2,1)}), bf16[8,96,1024]{2,1,0:T(8,128)(2,1)}, u32[]{:S(2)}, u32[]{:S(2)}) %all-to-all-start) | async-done | bytes 1572896 | tf_op jit(solution)/shard_map/all_to_all | solution.py:42
  61.5 96.2 %all_to_all.15 = bf16[2,1,1024,1344]{2,3,1,0:T(8,128)(2,1)S(1)} all-to-all(bf16[2,1,1024,1344]{2,3,1,0:T(8,128)(2,1)} %pad_maximum_fusion), channel_id=1, replica_groups=mesh['groups'=2,'expert'=8,'sub'=2] {'sub'}, dimensions={0} | all-to-all | bytes 11010048 | tf_op jit(solution)/shard_map/all_to_all | solution.py:10
  157.7 8.1 %multiply_convert_fusion = bf16[768,2688]{1,0:T(8,128)(2,1)} fusion(bf16[768,1024]{1,0:T(8,128)(2,1)} %bitcast.5, bf16[1024,2688]{0,1:T(8,128)(2,1)S(1)} %bitcast.27), kind=kOutput, calls=%fused_computation.3 | convolution fusion | flops 4234051584 | bytes 11206656 | tf_op jit(solution)/shard_map/dot_general | solution.py:15
  165.8 9.6 %fusion.2 = bf16[768,1024]{1,0:T(8,128)(2,1)} fusion(bf16[768,2688]{1,0:T(8,128)(2,1)} %multiply_convert_fusion, bf16[1,1024,2688]{1,2,0:T(8,128)(2,1)} %all-gather.2.cloned.1.call-done), kind=kOutput, calls=%fused_computation.8 | convolution fusion | flops 4228644864 | bytes 11206656 | tf_op jit(solution)/shard_map/dot_general | solution.py:17
  175.4 4.6 %all-to-all-start.2 = ((bf16[8,96,1024]{2,1,0:T(8,128)(2,1)}), bf16[8,96,1024]{2,1,0:T(8,128)(2,1)S(1)}, u32[]{:S(2)}, u32[]{:S(2)}) async-start(bf16[8,96,1024]{2,1,0:T(8,128)(2,1)} %bitcast.10), calls=%async_computation.2 | async-start | bytes 3145728 | tf_op jit(solution)/shard_map/all_to_all | solution.py:49
  180.0 0.1 copy.10
  180.1 37.7 %all-to-all-done.2 = bf16[8,96,1024]{2,1,0:T(8,128)(2,1)S(1)} async-done(((bf16[8,96,1024]{2,1,0:T(8,128)(2,1)}), bf16[8,96,1024]{2,1,0:T(8,128)(2,1)S(1)}, u32[]{:S(2)}, u32[]{:S(2)}) %all-to-all-start.2) | async-done | bytes 1572896 | tf_op jit(solution)/shard_map/all_to_all | solution.py:49
  217.8 2.0 gather_fusion.1
  219.9 0.7 reshape.72
  220.6 2.1 multiply_reduce_fusion
  (15 shorter events, 0.2 us)
Async XLA Ops:
  17.0 7.4 %copy-start = (bf16[1,1024,1344]{1,2,0:T(8,128)(2,1)S(1)}, bf16[1,1024,1344]{1,2,0:T(8,128)(2,1)}, u32[]{:S(2)}) copy-start(bf16[1,1024,1344]{1,2,0:T(8,128)(2,1)} %param.8) | copy-start | bytes 8257540
  17.0 44.5 %all-to-all-start = ((bf16[8,96,1024]{2,1,0:T(8,128)(2,1)}), bf16[8,96,1024]{2,1,0:T(8,128)(2,1)}, u32[]{:S(2)}, u32[]{:S(2)}) async-start(bf16[8,96,1024]{2,1,0:T(8,128)(2,1)} %bitcast.4), calls=%async_computation | async-start | bytes 3145728 | tf_op jit(solution)/shard_map/all_to_all | solution.py:42
  23.6 142.2 %all-gather.2.cloned.1.call-start = ((), (), s32[]{:S(2)}) async-start(), calls=%async_computation.3 | async-start | bytes 8257536 | tf_op jit(solution)/shard_map/all_gather | solution.py:47
  165.8 14.2 %copy-start.1 = (f32[128,4]{0,1:T(4,128)S(1)}, f32[128,4]{0,1:T(4,128)}, u32[]{:S(2)}) copy-start(f32[128,4]{0,1:T(4,128)} %param.7) | copy-start | bytes 6148
  175.4 42.4 %all-to-all-start.2 = ((bf16[8,96,1024]{2,1,0:T(8,128)(2,1)}), bf16[8,96,1024]{2,1,0:T(8,128)(2,1)S(1)}, u32[]{:S(2)}, u32[]{:S(2)}) async-start(bf16[8,96,1024]{2,1,0:T(8,128)(2,1)} %bitcast.10), calls=%async_computation.2 | async-start | bytes 3145728 | tf_op jit(solution)/shard_map/all_to_all | solution.py:49
Sparse Core Ops, SparseCore 0:
  26.0 103.2 all-gather.1
